TPU v7x, 32 devices: a whole 2x2x4 slice. The times are simulated.
32 devices in a mesh: cell: 2 (over core), gene: 4 (over y, x), rank: 4 (over z).
Axes of the slice: x: 2, y: 2, z: 4, core: 2. Of those that a mesh axis runs over, the one named last changes fastest.
Arguments:
- blocks: bfloat16 [2, 16, 96, 256, 128], P('cell', ('gene', 'rank')), may hold values from -6 to 6
- block_pos: int32 [2, 16, 96], P('cell', ('gene', 'rank')), may hold values from 0 to 127, as said below
- block_count: int32 [2, 16], P('cell', ('gene', 'rank')), may hold values from 32 to 96, as said below
- test_right: bfloat16 [32768, 512], P(('gene', 'rank')), may hold values from -0.0625 to 0.0625
- test_left: bfloat16 [4096, 768], P('cell', 'rank'), may hold values from -0.1875 to 0.1875
- gene_sketch_old: float32 [768, 32768], P('cell', ('gene', 'rank')), may hold values from -4 to 4
Outputs:
- right_sketch: float32 [4096, 512], P(('cell', 'gene', 'rank'))
- gene_sketch: float32 [768, 32768], P('cell', ('gene', 'rank'))
- core: float32 [768, 512], P('cell')
Inputs may be any that keep to these rules, and one draw needn't show every extreme that they name: `block_pos`: position p names row block p // 16 and gene block p % 16 of the device's tile; the 96 positions of one device are distinct. `block_count`: some device has all 96 slots live in every draw; slots from the count on are not part of A.
All inputs are finite; a program needn't handle non-finite values.
Results may differ from a plain program's by a relative error of at most 0.0003.
Values may be sent and summed in bfloat16 or wider, within the bound.
A program may use at most 128 MiB of HBM per device.

v0:
```python
import jax
import jax.numpy as jnp
from jax import lax
from jax.sharding import PartitionSpec as P

GROUP = 16


def body(blocks, block_pos, block_count, test_right, test_left, gene_sketch_old):
    highest = lax.Precision.HIGHEST
    tiles = blocks[0, 0]
    positions = block_pos[0, 0]
    live_count = block_count[0, 0]
    slots, block_rows, block_cols = tiles.shape
    gene_blocks = test_right.shape[0] // block_cols
    right_width = test_right.shape[1]
    left_full = lax.all_gather(test_left, "rank", axis=1, tiled=True)
    row_blocks = left_full.shape[0] // block_rows
    left_width = left_full.shape[1]
    right_table = test_right.reshape(gene_blocks, block_cols, right_width)
    left_table = left_full.reshape(row_blocks, block_rows, left_width)
    offsets = jnp.arange(GROUP, dtype=jnp.int32)

    def visit(turn_index, carry):
        right_acc, gene_acc = carry
        first_slot = turn_index * GROUP
        group_tiles = lax.dynamic_slice_in_dim(tiles, first_slot, GROUP, 0)
        group_places = lax.dynamic_slice_in_dim(positions, first_slot, GROUP, 0)
        alive_mask = (first_slot + offsets < live_count).astype(jnp.float32)
        row_block = group_places // gene_blocks
        gene_block = group_places % gene_blocks
        right_rows = jnp.take(right_table, gene_block, axis=0)
        left_rows = jnp.take(left_table, row_block, axis=0)
        right_terms = (
            jnp.einsum("pik,pkr->pir", group_tiles, right_rows, preferred_element_type=jnp.float32)
            * alive_mask[:, None, None]
        )
        gene_terms = (
            jnp.einsum("pil,pik->lpk", left_rows, group_tiles, preferred_element_type=jnp.float32)
            * alive_mask[None, :, None]
        )
        right_acc = right_acc.at[row_block].add(right_terms)
        gene_acc = gene_acc.at[:, gene_block].add(gene_terms)
        return (right_acc, gene_acc)

    turn_count = (live_count + GROUP - 1) // GROUP
    initial = (
        jnp.zeros((row_blocks, block_rows, right_width), jnp.float32),
        jnp.zeros((left_width, gene_blocks, block_cols), jnp.float32),
    )
    right_part, gene_part = lax.fori_loop(0, turn_count, visit, initial)
    right_flat = right_part.reshape(row_blocks * block_rows, right_width)
    gene_flat = gene_part.reshape(left_width, gene_blocks * block_cols)
    right_half = lax.psum_scatter(right_flat, "gene", scatter_dimension=0, tiled=True)
    right_mine = lax.psum_scatter(right_half, "rank", scatter_dimension=0, tiled=True)
    gene_mine = lax.psum_scatter(gene_flat, "cell", scatter_dimension=0, tiled=True)
    gene_sketch = gene_sketch_old + gene_mine
    shard_index = lax.axis_index("gene") * lax.axis_size("rank") + lax.axis_index("rank")
    mine_rows = right_mine.shape[0]
    left_mine = lax.dynamic_slice_in_dim(left_full, shard_index * mine_rows, mine_rows, 0).astype(
        jnp.float32
    )
    core_part = lax.dot_general(left_mine, right_mine, (((0,), (0,)), ((), ())), precision=highest)
    core_total = lax.psum(core_part, ("cell", "gene", "rank"))
    share = left_width // lax.axis_size("cell")
    core = lax.dynamic_slice_in_dim(core_total, lax.axis_index("cell") * share, share, 0)
    return (right_mine, gene_sketch, core)


def solution(mesh):
    return jax.shard_map(
        body,
        mesh=mesh,
        in_specs=(
            P("cell", ("gene", "rank"), None, None, None),
            P("cell", ("gene", "rank"), None),
            P("cell", ("gene", "rank")),
            P(("gene", "rank"), None),
            P("cell", "rank"),
            P("cell", ("gene", "rank")),
        ),
        out_specs=(P(("cell", "gene", "rank"), None), P("cell", ("gene", "rank")), P("cell", None)),
        check_vma=False,
    )
```

profile of v0, /device:TPU:0, one launch (start us, length us, event | category | flops | bytes accessed | tf_op | source)
XLA Modules:
  0.0 696.2 jit_solution(15199658908383752672)
XLA Ops:
  8.6 67.1 %all-gather.2.cloned.1.call-done = bf16[2048,768]{0,1:T(8,128)(2,1)} async-done(((bf16[2048,192]{0,1:T(8,128)(2,1)}), bf16[2048,768]{0,1:T(8,128)(2,1)}) %all-gather.2.cloned.1.call-update) | async-done | bytes 3145744 | tf_op jit(solution)/shard_map/all_gather | solution.py:17
  84.8 367.6 %while.15 = (s32[]{:T(128)}, f32[8,256,512]{2,1,0:T(8,128)}, f32[768,16,128]{2,0,1:T(8,128)}, s32[]{:T(128)}, s32[96]{0:T(128)S(1)}, /*index=5*/bf16[96,256,128]...) while((s32[]{:T(128)}, f32[8,256,512]{2,1,0:T(8,128)}, ...), condition=%wide.region_3.4_spmd.clone, body=%wide.region_0.3_spmd.clone.sunk | while | flops 1353714176 | bytes 98575488 | solution.py:51
  85.6 3.5 gather_fusion.1
  89.1 7.2 %multiply_bitcast_fusion.2 = f32[16,768,128]{1,2,0:T(8,128)} fusion(f32[16]{0:T(128)S(1)} %get-tuple-element.245, bf16[16,256,768]{2,1,0:T(8,128)(2,1)} %gather_fusion.1, pred[16]{0:T(512)(128)(4,1)S(1)} %get-tuple-element.249, bf16[96,256,128]{2,1,0:T(8,128)(2,1)} %get-tuple-element.281, s32[]{:T(128)S(6)} %select_n.101), kind=kOutput, calls=%fused_computation.5.clone.1 | convolution fusion | flops 810024960 | bytes 13631572 | tf_op jit(solution)/shard_map/while/body/pil,pik->lpk/dot_general | solution.py:39
  96.3 6.5 copy.17
  102.9 15.0 %scatter_fusion.1 = f32[768,16,128]{2,0,1:T(8,128)} fusion(f32[768,16,128]{2,0,1:T(8,128)} %get-tuple-element.265, s32[16]{0:T(128)S(1)} %get-tuple-element.247, f32[16,768,128]{2,1,0:T(8,128)} %copy.17), kind=kCustom, calls=%fused_computation.3.clone.clone.1 | custom fusion | flops 1572864 | bytes 18874432 | tf_op jit(solution)/shard_map/while/body/scatter-add | solution.py:43
  117.9 3.6 gather_fusion
  121.4 6.5 broadcast_multiply_fusion.2
  127.9 17.9 %scatter_fusion = f32[8,256,512]{2,1,0:T(8,128)} fusion(f32[8,256,512]{2,1,0:T(8,128)} %get-tuple-element.264, s32[16]{0:T(128)S(1)} %get-tuple-element.244, f32[16,256,512]{2,1,0:T(8,128)} %broadcast_multiply_fusion.2), kind=kCustom, calls=%fused_computation.2.clone.clone.1 | custom fusion | flops 2097152 | bytes 25165888 | tf_op jit(solution)/shard_map/while/body/scatter-add | solution.py:42
  146.6 3.5 gather_fusion.1
  150.1 7.2 %multiply_bitcast_fusion.2 = f32[16,768,128]{1,2,0:T(8,128)} fusion(f32[16]{0:T(128)S(1)} %get-tuple-element.245, bf16[16,256,768]{2,1,0:T(8,128)(2,1)} %gather_fusion.1, pred[16]{0:T(512)(128)(4,1)S(1)} %get-tuple-element.249, bf16[96,256,128]{2,1,0:T(8,128)(2,1)} %get-tuple-element.281, s32[]{:T(128)S(6)} %select_n.101), kind=kOutput, calls=%fused_computation.5.clone.1 | convolution fusion | flops 810024960 | bytes 13631572 | tf_op jit(solution)/shard_map/while/body/pil,pik->lpk/dot_general | solution.py:39
  157.3 6.5 copy.17
  163.9 15.3 %scatter_fusion.1 = f32[768,16,128]{2,0,1:T(8,128)} fusion(f32[768,16,128]{2,0,1:T(8,128)} %get-tuple-element.265, s32[16]{0:T(128)S(1)} %get-tuple-element.247, f32[16,768,128]{2,1,0:T(8,128)} %copy.17), kind=kCustom, calls=%fused_computation.3.clone.clone.1 | custom fusion | flops 1572864 | bytes 18874432 | tf_op jit(solution)/shard_map/while/body/scatter-add | solution.py:43
  179.2 3.6 gather_fusion
  182.8 6.5 broadcast_multiply_fusion.2
  189.2 17.7 %scatter_fusion = f32[8,256,512]{2,1,0:T(8,128)} fusion(f32[8,256,512]{2,1,0:T(8,128)} %get-tuple-element.264, s32[16]{0:T(128)S(1)} %get-tuple-element.244, f32[16,256,512]{2,1,0:T(8,128)} %broadcast_multiply_fusion.2), kind=kCustom, calls=%fused_computation.2.clone.clone.1 | custom fusion | flops 2097152 | bytes 25165888 | tf_op jit(solution)/shard_map/while/body/scatter-add | solution.py:42
  207.7 3.5 gather_fusion.1
  211.2 7.2 %multiply_bitcast_fusion.2 = f32[16,768,128]{1,2,0:T(8,128)} fusion(f32[16]{0:T(128)S(1)} %get-tuple-element.245, bf16[16,256,768]{2,1,0:T(8,128)(2,1)} %gather_fusion.1, pred[16]{0:T(512)(128)(4,1)S(1)} %get-tuple-element.249, bf16[96,256,128]{2,1,0:T(8,128)(2,1)} %get-tuple-element.281, s32[]{:T(128)S(6)} %select_n.101), kind=kOutput, calls=%fused_computation.5.clone.1 | convolution fusion | flops 810024960 | bytes 13631572 | tf_op jit(solution)/shard_map/while/body/pil,pik->lpk/dot_general | solution.py:39
  218.4 6.5 copy.17
  225.0 15.3 %scatter_fusion.1 = f32[768,16,128]{2,0,1:T(8,128)} fusion(f32[768,16,128]{2,0,1:T(8,128)} %get-tuple-element.265, s32[16]{0:T(128)S(1)} %get-tuple-element.247, f32[16,768,128]{2,1,0:T(8,128)} %copy.17), kind=kCustom, calls=%fused_computation.3.clone.clone.1 | custom fusion | flops 1572864 | bytes 18874432 | tf_op jit(solution)/shard_map/while/body/scatter-add | solution.py:43
  240.3 3.6 gather_fusion
  243.9 6.5 broadcast_multiply_fusion.2
  250.3 18.4 %scatter_fusion = f32[8,256,512]{2,1,0:T(8,128)} fusion(f32[8,256,512]{2,1,0:T(8,128)} %get-tuple-element.264, s32[16]{0:T(128)S(1)} %get-tuple-element.244, f32[16,256,512]{2,1,0:T(8,128)} %broadcast_multiply_fusion.2), kind=kCustom, calls=%fused_computation.2.clone.clone.1 | custom fusion | flops 2097152 | bytes 25165888 | tf_op jit(solution)/shard_map/while/body/scatter-add | solution.py:42
  273.0 7.2 %multiply_bitcast_fusion.2 = f32[16,768,128]{1,2,0:T(8,128)} fusion(f32[16]{0:T(128)S(1)} %get-tuple-element.245, bf16[16,256,768]{2,1,0:T(8,128)(2,1)} %gather_fusion.1, pred[16]{0:T(512)(128)(4,1)S(1)} %get-tuple-element.249, bf16[96,256,128]{2,1,0:T(8,128)(2,1)} %get-tuple-element.281, s32[]{:T(128)S(6)} %select_n.101), kind=kOutput, calls=%fused_computation.5.clone.1 | convolution fusion | flops 810024960 | bytes 13631572 | tf_op jit(solution)/shard_map/while/body/pil,pik->lpk/dot_general | solution.py:39
  280.2 6.5 copy.17
  286.8 15.3 %scatter_fusion.1 = f32[768,16,128]{2,0,1:T(8,128)} fusion(f32[768,16,128]{2,0,1:T(8,128)} %get-tuple-element.265, s32[16]{0:T(128)S(1)} %get-tuple-element.247, f32[16,768,128]{2,1,0:T(8,128)} %copy.17), kind=kCustom, calls=%fused_computation.3.clone.clone.1 | custom fusion | flops 1572864 | bytes 18874432 | tf_op jit(solution)/shard_map/while/body/scatter-add | solution.py:43
  302.0 3.6 gather_fusion
  305.6 6.5 broadcast_multiply_fusion.2
  312.1 18.1 %scatter_fusion = f32[8,256,512]{2,1,0:T(8,128)} fusion(f32[8,256,512]{2,1,0:T(8,128)} %get-tuple-element.264, s32[16]{0:T(128)S(1)} %get-tuple-element.244, f32[16,256,512]{2,1,0:T(8,128)} %broadcast_multiply_fusion.2), kind=kCustom, calls=%fused_computation.2.clone.clone.1 | custom fusion | flops 2097152 | bytes 25165888 | tf_op jit(solution)/shard_map/while/body/scatter-add | solution.py:42
  330.9 3.5 gather_fusion.1
  334.5 7.2 %multiply_bitcast_fusion.2 = f32[16,768,128]{1,2,0:T(8,128)} fusion(f32[16]{0:T(128)S(1)} %get-tuple-element.245, bf16[16,256,768]{2,1,0:T(8,128)(2,1)} %gather_fusion.1, pred[16]{0:T(512)(128)(4,1)S(1)} %get-tuple-element.249, bf16[96,256,128]{2,1,0:T(8,128)(2,1)} %get-tuple-element.281, s32[]{:T(128)S(6)} %select_n.101), kind=kOutput, calls=%fused_computation.5.clone.1 | convolution fusion | flops 810024960 | bytes 13631572 | tf_op jit(solution)/shard_map/while/body/pil,pik->lpk/dot_general | solution.py:39
  341.6 6.5 copy.17
  348.2 15.2 %scatter_fusion.1 = f32[768,16,128]{2,0,1:T(8,128)} fusion(f32[768,16,128]{2,0,1:T(8,128)} %get-tuple-element.265, s32[16]{0:T(128)S(1)} %get-tuple-element.247, f32[16,768,128]{2,1,0:T(8,128)} %copy.17), kind=kCustom, calls=%fused_computation.3.clone.clone.1 | custom fusion | flops 1572864 | bytes 18874432 | tf_op jit(solution)/shard_map/while/body/scatter-add | solution.py:43
  363.4 3.6 gather_fusion
  367.0 6.5 broadcast_multiply_fusion.2
  373.5 17.9 %scatter_fusion = f32[8,256,512]{2,1,0:T(8,128)} fusion(f32[8,256,512]{2,1,0:T(8,128)} %get-tuple-element.264, s32[16]{0:T(128)S(1)} %get-tuple-element.244, f32[16,256,512]{2,1,0:T(8,128)} %broadcast_multiply_fusion.2), kind=kCustom, calls=%fused_computation.2.clone.clone.1 | custom fusion | flops 2097152 | bytes 25165888 | tf_op jit(solution)/shard_map/while/body/scatter-add | solution.py:42
  395.7 7.2 %multiply_bitcast_fusion.2 = f32[16,768,128]{1,2,0:T(8,128)} fusion(f32[16]{0:T(128)S(1)} %get-tuple-element.245, bf16[16,256,768]{2,1,0:T(8,128)(2,1)} %gather_fusion.1, pred[16]{0:T(512)(128)(4,1)S(1)} %get-tuple-element.249, bf16[96,256,128]{2,1,0:T(8,128)(2,1)} %get-tuple-element.281, s32[]{:T(128)S(6)} %select_n.101), kind=kOutput, calls=%fused_computation.5.clone.1 | convolution fusion | flops 810024960 | bytes 13631572 | tf_op jit(solution)/shard_map/while/body/pil,pik->lpk/dot_general | solution.py:39
  402.9 6.5 copy.17
  409.4 15.3 %scatter_fusion.1 = f32[768,16,128]{2,0,1:T(8,128)} fusion(f32[768,16,128]{2,0,1:T(8,128)} %get-tuple-element.265, s32[16]{0:T(128)S(1)} %get-tuple-element.247, f32[16,768,128]{2,1,0:T(8,128)} %copy.17), kind=kCustom, calls=%fused_computation.3.clone.clone.1 | custom fusion | flops 1572864 | bytes 18874432 | tf_op jit(solution)/shard_map/while/body/scatter-add | solution.py:43
  424.7 3.6 gather_fusion
  428.3 6.5 broadcast_multiply_fusion.2
  434.8 17.7 %scatter_fusion = f32[8,256,512]{2,1,0:T(8,128)} fusion(f32[8,256,512]{2,1,0:T(8,128)} %get-tuple-element.264, s32[16]{0:T(128)S(1)} %get-tuple-element.244, f32[16,256,512]{2,1,0:T(8,128)} %broadcast_multiply_fusion.2), kind=kCustom, calls=%fused_computation.2.clone.clone.1 | custom fusion | flops 2097152 | bytes 25165888 | tf_op jit(solution)/shard_map/while/body/scatter-add | solution.py:42
  452.5 50.9 %reduce-scatter.4.cloned.1.call-done = f32[512,512]{1,0:T(8,128)} async-done(((f32[2048,512]{1,0:T(8,128)}), f32[512,512]{1,0:T(8,128)}) %reduce-scatter.4.cloned.1.call-update) | async-done | bytes 1048592 | tf_op jit(solution)/shard_map/reduce_scatter | solution.py:54
  503.5 30.1 %reduce-scatter.6.cloned.1.call-done = f32[128,512]{1,0:T(8,128)} async-done(((f32[512,512]{1,0:T(8,128)}), f32[128,512]{1,0:T(8,128)}) %reduce-scatter.6.cloned.1.call-update) | async-done | bytes 262160 | tf_op jit(solution)/shard_map/reduce_scatter | solution.py:55
  536.7 6.3 copy_bitcast_fusion
  543.1 127.4 %all-reduce.2.cloned.1.call-done = f32[768,512]{1,0:T(8,128)} async-done(((f32[768,512]{1,0:T(8,128)}), f32[768,512]{1,0:T(8,128)}) %all-reduce.2.cloned.1.call-update) | async-done | bytes 1572880 | tf_op jit(solution)/shard_map/psum | solution.py:64
  672.5 13.1 %reduce-scatter.8.cloned.1.call-done = f32[384,2048]{1,0:T(8,128)} async-done(((f32[768,2048]{1,0:T(8,128)}), f32[384,2048]{1,0:T(8,128)}) %reduce-scatter.8.cloned.1.call-update) | async-done | bytes 3145744 | tf_op jit(solution)/shard_map/reduce_scatter | solution.py:56
  685.6 4.0 add.91
  (45 shorter events, 26.7 us)
Async XLA Ops:
  7.2 68.6 %all-gather.2.cloned.1.call-start = ((), (), s32[]{:S(2)}) async-start(), calls=%async_computation.3 | async-start | bytes 3932160 | tf_op jit(solution)/shard_map/all_gather | solution.py:17
  7.9 495.6 %reduce-scatter.4.cloned.1.call-start = ((), (), s32[]{:S(2)}) async-start(), calls=%async_computation.4 | async-start | bytes 5242880 | tf_op jit(solution)/shard_map/reduce_scatter | solution.py:54
  78.9 5.9 copy-start.1
  452.5 81.2 %reduce-scatter.6.cloned.1.call-start = ((), (), s32[]{:S(2)}) async-start(), calls=%async_computation.5 | async-start | bytes 1310720 | tf_op jit(solution)/shard_map/reduce_scatter | solution.py:55
  503.5 167.0 %all-reduce.2.cloned.1.call-start = ((), (), s32[]{:S(2)}) async-start(), calls=%async_computation.7 | async-start | bytes 3145728 | tf_op jit(solution)/shard_map/psum | solution.py:64
  536.7 148.9 %reduce-scatter.8.cloned.1.call-start = ((), (), s32[]{:S(2)}) async-start(), calls=%async_computation.6 | async-start | bytes 9437184 | tf_op jit(solution)/shard_map/reduce_scatter | solution.py:56
  543.0 142.6 %copy-start = (f32[384,2048]{1,0:T(8,128)S(1)}, f32[384,2048]{1,0:T(8,128)}, u32[]{:S(2)}) copy-start(f32[384,2048]{1,0:T(8,128)} %param.13) | copy-start | bytes 9437188
Sparse Core Ops, SparseCore 0:
  9.5 66.1 all-gather.1
  452.6 50.8 reduce-scatter.3
  506.3 27.2 reduce-scatter.5
  539.4 131.0 all-reduce.1
  672.6 12.9 reduce-scatter.7
where the time goes:
time: 698 us; the launch traced here: 696 us
  waiting for transfers between devices  289 us (41%)
  other arithmetic  208 us (30%)
  local copies, waits for them, and re-layouts  99.5 us (14%)
  matrix products  84.9 us (12%)
  between operations  14.5 us (2%)
    psum x1, waiting for transfers between devices, body(): core_total = lax.psum(core_part, ('cell', 'gene', 'rank'))  127 us
    scatter-add x6, other arithmetic, visit(): right_acc = right_acc.at[row_block].add(right_terms)  108 us
    scatter-add x6, other arithmetic, visit(): gene_acc = gene_acc.at[:, gene_block].add(gene_terms)  91.4 us
    all_gather x1, waiting for transfers between devices, body(): left_full = lax.all_gather(test_left, 'rank', axis=1, tiled=True)  67.1 us
    reduce_scatter x1, waiting for transfers between devices, body(): lax.psum_scatter(right_flat, 'gene', scatter_dimension=0, tiled=True)  50.9 us
    dot_general x6, matrix products, visit(): jnp.einsum('pil,pik->lpk', left_rows, group_tiles, preferred_element_type...  43.1 us
    mul x6, local copies, waits for them, and re-layouts, visit(): jnp.einsum('pil,pik->lpk', left_rows, group_tiles, preferred_element_type...  39.3 us
    dot_general x6, matrix products, visit(): jnp.einsum('pik,pkr->pir', group_tiles, right_rows, preferred_element_typ...  38.8 us
  transfers between devices with their start and end apart: 5, of which 5 were waited for; matrix products, arithmetic and copies ran while one was open for 1% of the time, Pallas kernels for 0%

commit v1 on v0

v1 whole, which is shorter than its diff:
```python
import functools

import jax
import jax.numpy as jnp
from jax import lax
from jax.experimental import pallas as pl
from jax.experimental.pallas import tpu as pltpu
from jax.sharding import PartitionSpec as P

MESH = pl.DeviceIdType.MESH
GENE_CHUNK = 256


def kernel(
    sizes, code, blocks, right_in, left_in, right_out, gene_out, core_out,
    tiles, dense, table, left, part, hop1, hop2, hopz,
    core_part, core_cell, core_gene, core_rank, gene_send, gene_recv,
    load_sem, agz_s, agz_r, agx_s, agx_r, rs1_s, rs1_r, rs2_s, rs2_r, rsz_s, rsz_r,
    cc_s, cc_r, cg_s, cg_r, cr_s, cr_r, ar_s, ar_r, ag_s, ag_r, gs_s, gs_r,
):
    n_cell, n_gene, n_rank = sizes
    f32, bf16 = jnp.float32, jnp.bfloat16
    c, g, r = lax.axis_index("cell"), lax.axis_index("gene"), lax.axis_index("rank")
    b1, b0 = g // 2, g % 2
    gx = 2 * b1 + (1 - b0)
    gy = 2 * (1 - b1) + b0
    gd = 2 * (1 - b1) + (1 - b0)
    gene_peers = [gx, gy, gd]
    rows, width = part.shape
    quarter = rows // n_gene
    shard = quarter // n_rank
    half = width // 2
    lw = left_in.shape[0]
    left_width = left.shape[0]
    brows, bcols = tiles.shape[1], tiles.shape[2]
    gene_blocks = dense.shape[1] // bcols
    share = left_width // n_cell
    core_rows = share // n_gene
    lanes = width // n_rank

    def rank_of(k):
        return lax.rem(r + k, n_rank)

    def cell_of(k):
        return lax.rem(c + k, n_cell)

    def cut(start, step):
        return pl.ds(pl.multiple_of(start * step, step), step)

    def remote(src, dst, ssem, rsem, **where):
        device = (where.get("cell", c), where.get("gene", g), where.get("rank", r))
        return pltpu.make_async_remote_copy(
            src_ref=src, dst_ref=dst, send_sem=ssem, recv_sem=rsem,
            device_id=device, device_id_type=MESH,
        )

    barrier = pltpu.get_barrier_semaphore()
    for k in range(1, n_rank):
        pl.semaphore_signal(barrier, inc=1, device_id=(c, g, rank_of(k)), device_id_type=MESH)
    for peer in gene_peers:
        pl.semaphore_signal(barrier, inc=1, device_id=(c, peer, r), device_id_type=MESH)
    for k in range(1, n_cell):
        pl.semaphore_signal(barrier, inc=1, device_id=(cell_of(k), g, r), device_id_type=MESH)

    load_tiles = pltpu.make_async_copy(blocks, tiles, load_sem.at[0])
    load_table = pltpu.make_async_copy(right_in, table, load_sem.at[1])
    load_tiles.start()
    load_table.start()
    own_left = []
    for i, q in enumerate((g, gd)):
        copy = pltpu.make_async_copy(
            left_in.at[:, cut(q, quarter)], left.at[cut(r, lw), cut(q, quarter)], load_sem.at[2 + i]
        )
        copy.start()
        own_left.append(copy)

    pl.semaphore_wait(barrier, (n_rank - 1) + len(gene_peers) + (n_cell - 1))

    agz = []
    for i, q in enumerate((g, gd)):
        for k in range(1, n_rank):
            s = i * (n_rank - 1) + k - 1
            copy = remote(
                left_in.at[:, cut(q, quarter)], left.at[cut(r, lw), cut(q, quarter)],
                agz_s.at[s], agz_r.at[s], rank=rank_of(k),
            )
            copy.start()
            agz.append(copy)
    load_tiles.wait()
    load_table.wait()

    row_blocks = quarter // brows

    def compute(q):
        def fill(i, carry):
            rb = q * row_blocks + i // gene_blocks
            gb = i % gene_blocks
            slot = code[rb * gene_blocks + gb]
            block = tiles[jnp.maximum(slot - 1, 0)]
            dense[cut(rb, brows), cut(gb, bcols)] = jnp.where(slot > 0, block, jnp.zeros_like(block))
            return carry

        lax.fori_loop(0, row_blocks * gene_blocks, fill, 0)

        def multiply(h, carry):
            part[cut(q, quarter), cut(h, half)] = jnp.dot(
                dense[cut(q, quarter), :], table[:, cut(h, half)], preferred_element_type=f32
            )
            return carry

        lax.fori_loop(0, 2, multiply, 0)

    h0, h1 = pl.ds(0, half), pl.ds(half, half)

    def rs1(i, q, h, peer):
        copy = remote(part.at[cut(q, quarter), h], hop1.at[i], rs1_s.at[i], rs1_r.at[i], gene=peer)
        copy.start()
        return copy

    compute(gd)
    d0 = rs1(0, gd, h0, gx)
    d1 = rs1(1, gd, h1, gy)
    compute(gx)
    o0 = rs1(2, gx, h0, gx)
    compute(gy)
    o1 = rs1(3, gy, h1, gy)
    compute(g)

    order = [rank_of(k) for k in range(1, n_rank)] + [r]
    second = []
    for i, (first, q, h, peer) in enumerate(((d0, gy, h0, gy), (d1, gx, h1, gx))):
        first.wait_recv()
        copies = []
        for j, z in enumerate(order):
            here = pl.ds(pl.multiple_of(q * quarter + z * shard, shard), shard)
            part[here, h] = part[here, h] + hop1[i, cut(z, shard), :]
            copy = remote(
                part.at[here, h], hop2.at[i, cut(z, shard), :],
                rs2_s.at[i * n_rank + j], rs2_r.at[i * n_rank + j], gene=peer,
            )
            copy.start()
            copies.append(copy)
        second.append(copies)

    for copy in own_left:
        copy.wait()
    for copy in agz[: n_rank - 1]:
        copy.wait_recv()
    agx = []
    for i, peer in enumerate((gx, gy)):
        copy = remote(
            left.at[:, cut(g, quarter)], left.at[:, cut(g, quarter)], agx_s.at[i], agx_r.at[i], gene=peer
        )
        copy.start()
        agx.append(copy)

    o0.wait_recv()
    o1.wait_recv()
    rsz = []
    for j, z in enumerate(order):
        second[0][j].wait_recv()
        second[1][j].wait_recv()
        here = pl.ds(pl.multiple_of(g * quarter + z * shard, shard), shard)
        part[here, h0] = part[here, h0] + hop1[2, cut(z, shard), :] + hop2[0, cut(z, shard), :]
        part[here, h1] = part[here, h1] + hop1[3, cut(z, shard), :] + hop2[1, cut(z, shard), :]
        if j < n_rank - 1:
            copy = remote(part.at[here, :], hopz.at[j], rsz_s.at[j], rsz_r.at[j], rank=z)
            copy.start()
            rsz.append(copy)
    for copy in rsz:
        copy.wait_recv()
    mine_at = pl.ds(pl.multiple_of(g * quarter + r * shard, shard), shard)
    mine = part[mine_at, :]
    for j in range(n_rank - 1):
        mine = mine + hopz[j]
    right_out[...] = mine

    hi = mine.astype(bf16)
    rest = mine - hi.astype(f32)
    mid = rest.astype(bf16)
    low = (rest - mid.astype(f32)).astype(bf16)
    left_mine = left[:, mine_at]
    core_part[...] = (
        jnp.dot(left_mine, hi, preferred_element_type=f32)
        + jnp.dot(left_mine, mid, preferred_element_type=f32)
        + jnp.dot(left_mine, low, preferred_element_type=f32)
    )
    own_share = cut(c, share)
    cc = []
    for k in range(1, n_cell):
        copy = remote(
            core_part.at[cut(cell_of(k), share), :], core_cell.at[k - 1],
            cc_s.at[k - 1], cc_r.at[k - 1], cell=cell_of(k),
        )
        copy.start()
        cc.append(copy)
    for k in range(1, n_cell):
        cc[k - 1].wait_recv()
        core_part[own_share, :] = core_part[own_share, :] + core_cell[k - 1]
    cg = []
    for i, peer in enumerate(gene_peers):
        src = pl.ds(pl.multiple_of(c * share + peer * core_rows, 8), core_rows)
        copy = remote(core_part.at[src, :], core_gene.at[i], cg_s.at[i], cg_r.at[i], gene=peer)
        copy.start()
        cg.append(copy)

    for copy in agz[n_rank - 1 :]:
        copy.wait_recv()
    for copy in agx:
        copy.wait_recv()
    chunks = dense.shape[1] // GENE_CHUNK

    def gene_copy(k, j):
        return remote(
            gene_send.at[k - 1, :, cut(j, GENE_CHUNK)], gene_recv.at[k - 1, :, cut(j, GENE_CHUNK)],
            gs_s.at[k - 1, j], gs_r.at[k - 1, j], cell=cell_of(k),
        )

    for k in range(1, n_cell):
        peer_rows = cut(cell_of(k), share)

        def send_chunk(j, carry):
            gene_send[k - 1, :, cut(j, GENE_CHUNK)] = jnp.dot(
                left[peer_rows, :], dense[:, cut(j, GENE_CHUNK)], preferred_element_type=f32
            )
            gene_copy(k, j).start()
            return carry

        lax.fori_loop(0, chunks, send_chunk, 0)

    own_rows = pl.ds(pl.multiple_of(c * share + g * core_rows, 8), core_rows)
    for i in range(len(gene_peers)):
        cg[i].wait_recv()
        core_part[own_rows, :] = core_part[own_rows, :] + core_gene[i]
    cr = []
    for k in range(1, n_rank):
        copy = remote(
            core_part.at[own_rows, cut(rank_of(k), lanes)], core_rank.at[k - 1],
            cr_s.at[k - 1], cr_r.at[k - 1], rank=rank_of(k),
        )
        copy.start()
        cr.append(copy)

    def own_chunk(j, carry):
        gene_out[:, cut(j, GENE_CHUNK)] = jnp.dot(
            left[own_share, :], dense[:, cut(j, GENE_CHUNK)], preferred_element_type=f32
        )
        return carry

    lax.fori_loop(0, chunks // 2, own_chunk, 0)

    final = core_part[own_rows, cut(r, lanes)]
    for k in range(1, n_rank):
        cr[k - 1].wait_recv()
        final = final + core_rank[k - 1]
    out_rows = pl.ds(pl.multiple_of(g * core_rows, 8), core_rows)
    core_out[out_rows, cut(r, lanes)] = final
    ar = []
    for k in range(1, n_rank):
        copy = remote(
            core_out.at[out_rows, cut(r, lanes)], core_out.at[out_rows, cut(r, lanes)],
            ar_s.at[k - 1], ar_r.at[k - 1], rank=rank_of(k),
        )
        copy.start()
        ar.append(copy)

    lax.fori_loop(chunks // 2, chunks, own_chunk, 0)

    for copy in ar:
        copy.wait_recv()
    ag = []
    for i, peer in enumerate(gene_peers):
        copy = remote(core_out.at[out_rows, :], core_out.at[out_rows, :], ag_s.at[i], ag_r.at[i], gene=peer)
        copy.start()
        ag.append(copy)

    for k in range(1, n_cell):

        def add_chunk(j, carry):
            gene_copy(k, j).wait_recv()
            here = cut(j, GENE_CHUNK)
            gene_out[:, here] = gene_out[:, here] + gene_recv[k - 1, :, here]
            return carry

        lax.fori_loop(0, chunks, add_chunk, 0)

    for copy in ag:
        copy.wait_recv()

    for copy in agz + agx + [d0, d1, o0, o1] + second[0] + second[1] + rsz + cc + cg + cr + ar + ag:
        copy.wait_send()
    for k in range(1, n_cell):

        def drain(j, carry):
            gene_copy(k, j).wait_send()
            return carry

        lax.fori_loop(0, chunks, drain, 0)


def body(sizes, blocks, block_pos, block_count, test_right, test_left, gene_sketch_old):
    n_cell, n_gene, n_rank = sizes
    f32, bf16 = jnp.float32, jnp.bfloat16
    tiles = blocks[0, 0]
    slots, brows, bcols = tiles.shape
    genes, width = test_right.shape
    rows, lw = test_left.shape
    left_width = lw * n_rank
    gene_blocks = genes // bcols
    places = (rows // brows) * gene_blocks
    slot_ids = jnp.arange(slots, dtype=jnp.int32)
    hit = (block_pos[0, 0][None, :] == jnp.arange(places, dtype=jnp.int32)[:, None]) & (
        slot_ids < block_count[0, 0]
    )[None, :]
    code = jnp.sum(jnp.where(hit, slot_ids[None, :] + 1, 0), axis=1).astype(jnp.int32)
    quarter, half = rows // n_gene, width // 2
    shard = quarter // n_rank
    share = left_width // n_cell
    core_rows, lanes = share // n_gene, width // n_rank
    chunks = genes // GENE_CHUNK
    dma = pltpu.SemaphoreType.DMA
    z, x = n_rank - 1, n_gene - 1

    def pair(*shape):
        return [dma(shape), dma(shape)]

    right_mine, gene_sum, core = pl.pallas_call(
        functools.partial(kernel, sizes),
        out_shape=(
            jax.ShapeDtypeStruct((shard, width), f32),
            jax.ShapeDtypeStruct((share, genes), f32),
            jax.ShapeDtypeStruct((share, width), f32),
        ),
        in_specs=[
            pl.BlockSpec(memory_space=pltpu.SMEM),
            pl.BlockSpec(memory_space=pl.ANY),
            pl.BlockSpec(memory_space=pl.ANY),
            pl.BlockSpec(memory_space=pl.ANY),
        ],
        out_specs=tuple(pl.BlockSpec(memory_space=pltpu.VMEM) for _ in range(3)),
        scratch_shapes=[
            pltpu.VMEM((slots, brows, bcols), bf16),
            pltpu.VMEM((rows, genes), bf16),
            pltpu.VMEM((genes, width), bf16),
            pltpu.VMEM((left_width, rows), bf16),
            pltpu.VMEM((rows, width), f32),
            pltpu.VMEM((4, quarter, half), f32),
            pltpu.VMEM((2, quarter, half), f32),
            pltpu.VMEM((z, shard, width), f32),
            pltpu.VMEM((left_width, width), f32),
            pltpu.VMEM((n_cell - 1, share, width), f32),
            pltpu.VMEM((x, core_rows, width), f32),
            pltpu.VMEM((z, core_rows, lanes), f32),
            pltpu.VMEM((n_cell - 1, share, genes), f32),
            pltpu.VMEM((n_cell - 1, share, genes), f32),
            dma((4,)),
            *pair(2 * z),
            *pair(2),
            *pair(4),
            *pair(2 * n_rank),
            *pair(z),
            *pair(n_cell - 1),
            *pair(x),
            *pair(z),
            *pair(z),
            *pair(x),
            *pair(n_cell - 1, chunks),
        ],
        compiler_params=pltpu.CompilerParams(
            collective_id=0, has_side_effects=True, vmem_limit_bytes=62 * 1024 * 1024
        ),
        name="sketch",
    )(code, tiles, test_right, test_left.T)
    return right_mine, gene_sketch_old + gene_sum, core


def solution(mesh):
    sizes = tuple(mesh.shape[name] for name in ("cell", "gene", "rank"))
    return jax.shard_map(
        functools.partial(body, sizes),
        mesh=mesh,
        in_specs=(
            P("cell", ("gene", "rank"), None, None, None),
            P("cell", ("gene", "rank"), None),
            P("cell", ("gene", "rank")),
            P(("gene", "rank"), None),
            P("cell", "rank"),
            P("cell", ("gene", "rank")),
        ),
        out_specs=(P(("cell", "gene", "rank"), None), P("cell", ("gene", "rank")), P("cell", None)),
        check_vma=False,
    )
```

time: 698 us -> 110 us (0.16)
  waiting for transfers between devices: 289 us -> 0 us
  other arithmetic: 208 us -> 6.57 us
  Pallas kernels: 0 us -> 101 us
  local copies, waits for them, and re-layouts: 99.5 us -> 1.59 us
  matrix products: 84.9 us -> 0 us
  between operations: 14.5 us -> 1.32 us
    scatter-add x12 -> x0, other arithmetic: 199 us -> none  [the longest x6 108 us: visit(): right_acc = right_acc.at[row_block].add(right_terms)]
    psum x1 -> x0, waiting for transfers between devices: 127 us -> none  [body(): core_total = lax.psum(core_part, ('cell', 'gene', 'rank'))]
    pallas_call x0 -> x1, Pallas kernels: none -> 101 us  [body(): pl.pallas_call(functools.partial(kernel, sizes), out_shape=(jax.ShapeDtyp...]
    reduce_scatter x3 -> x0, waiting for transfers between devices: 94.1 us -> none  [the longest x1 50.9 us: body(): lax.psum_scatter(right_flat, 'gene', scatter_dimension=0, tiled=True)]
    dot_general x13 -> x0, matrix products: 84.9 us -> none  [the longest x6 43.1 us: visit(): jnp.einsum('pil,pik->lpk', left_rows, group_tiles, preferred_element_type...]
    all_gather x1 -> x0, waiting for transfers between devices: 67.1 us -> none  [body(): left_full = lax.all_gather(test_left, 'rank', axis=1, tiled=True)]
    gather x12 -> x0, local copies, waits for them, and re-layouts: 42.8 us -> none  [the longest x6 21.5 us: visit(): right_rows = jnp.take(right_table, gene_block, axis=0)]
    mul x6 -> x0, local copies, waits for them, and re-layouts: 39.3 us -> none  [visit(): jnp.einsum('pil,pik->lpk', left_rows, group_tiles, preferred_element_type...]
  transfers between devices with their start and end apart: 5 -> 0, of which waited for: 5 -> 0; matrix products, arithmetic and copies ran while one was open for 1% -> 0% of each run, Pallas kernels for 0% -> 0%
where the time goes in v1:
time: 110 us
  Pallas kernels  101 us (92%)
  other arithmetic  6.57 us (6%)
  local copies, waits for them, and re-layouts  1.59 us (1%)
  between operations  1.32 us (1%)
    pallas_call x1, Pallas kernels, body(): pl.pallas_call(functools.partial(kernel, sizes), out_shape=(jax.ShapeDtyp...  101 us
    add x1, other arithmetic, body(): return (right_mine, gene_sketch_old + gene_sum, core)  5.27 us

profile of v1, /device:TPU:0, one launch (start us, length us, event | category | flops | bytes accessed | tf_op | source)
XLA Modules:
  0.0 110.2 jit_solution(13823773818895493524)
XLA Ops:
  1.3 1.3 %select_reduce_fusion.code = s32[128]{0:T(128)} fusion(s32[96]{0:T(128)S(1)} %iota_add_fusion, s32[96]{0:T(128)} %bitcast.7, pred[96]{0:T(512)(128)(4,1)S(1)} %iota_compare_fusion.1), kind=kLoop, calls=%fused_computation | loop fusion | flops 49024 | bytes 1376 | tf_op jit(solution)/shard_map/reduce_sum | solution.py:315
  2.6 100.7 %sketch.1 = (f32[128,512]{1,0:T(8,128)}, f32[384,2048]{1,0:T(8,128)}, f32[384,512]{1,0:T(8,128)}) custom-call(s32[128]{0:T(128)} %select_reduce_fusion.code, bf16[96,256,128]{2,1,0:T(8,128)(2,1)} %bitcast.5, bf16[2048,512]{1,0:T(8,128)(2,1)} %right_in.1, bf16[192,2048]{1,0:T(8,128)(2,1)} %bitcast.6), custom_call_target="tpu_custom_call" | custom-call | tf_op jit(solution)/shard_map/sketch/pallas_call | solution.py:327
  103.3 0.0 copy-start.1
  103.3 0.0 copy-start
  103.3 5.3 %add.16 = f32[384,2048]{1,0:T(8,128)} add(f32[384,2048]{1,0:T(8,128)} %param.11, f32[384,2048]{1,0:T(8,128)} %get-tuple-element.7) | non-fusion elementwise | flops 786432 | bytes 9437184 | tf_op jit(solution)/shard_map/add | solution.py:374
  108.6 0.0 copy-done.1
  108.6 0.7 copy.12
  109.3 0.0 copy-done
  109.3 0.9 copy.13
  (2 shorter events, 0.0 us)
Async XLA Ops:
  103.3 5.3 %copy-start.1 = (f32[128,512]{1,0:T(8,128)S(1)}, f32[128,512]{1,0:T(8,128)}, u32[]{:S(2)}) copy-start(f32[128,512]{1,0:T(8,128)} %get-tuple-element.12) | copy-start | bytes 786436
  103.3 6.0 %copy-start = (f32[384,512]{1,0:T(8,128)S(1)}, f32[384,512]{1,0:T(8,128)}, u32[]{:S(2)}) copy-start(f32[384,512]{1,0:T(8,128)} %get-tuple-element.14) | copy-start | bytes 2359300

commit v2 on v1

--- a/solution.py
+++ b/solution.py
@@ -147,12 +147,16 @@
     for copy in agz[: n_rank - 1]:
         copy.wait_recv()
     agx = []
-    for i, peer in enumerate((gx, gy)):
-        copy = remote(
-            left.at[:, cut(g, quarter)], left.at[:, cut(g, quarter)], agx_s.at[i], agx_r.at[i], gene=peer
-        )
-        copy.start()
-        agx.append(copy)
+
+    def send_left(k):
+        for i, peer in enumerate((gx, gy)):
+            here = left.at[cut(cell_of(k), share), cut(g, quarter)]
+            copy = remote(here, here, agx_s.at[k, i], agx_r.at[k, i], gene=peer)
+            copy.start()
+            agx.append(copy)
+
+    for k in range(1, n_cell):
+        send_left(k)
 
     o0.wait_recv()
     o1.wait_recv()
@@ -167,33 +171,37 @@
             copy = remote(part.at[here, :], hopz.at[j], rsz_s.at[j], rsz_r.at[j], rank=z)
             copy.start()
             rsz.append(copy)
-    for copy in rsz:
-        copy.wait_recv()
-    mine_at = pl.ds(pl.multiple_of(g * quarter + r * shard, shard), shard)
-    mine = part[mine_at, :]
-    for j in range(n_rank - 1):
-        mine = mine + hopz[j]
-    right_out[...] = mine
-
-    hi = mine.astype(bf16)
-    rest = mine - hi.astype(f32)
-    mid = rest.astype(bf16)
-    low = (rest - mid.astype(f32)).astype(bf16)
-    left_mine = left[:, mine_at]
-    core_part[...] = (
-        jnp.dot(left_mine, hi, preferred_element_type=f32)
-        + jnp.dot(left_mine, mid, preferred_element_type=f32)
-        + jnp.dot(left_mine, low, preferred_element_type=f32)
-    )
+    def core_rows_of(k):
+        at = cut(cell_of(k), share)
+
+        def multiply(h, carry):
+            here = cut(h, half)
+            mine = part[cut(g, quarter), here]
+            hi = mine.astype(bf16)
+            rest = mine - hi.astype(f32)
+            mid = rest.astype(bf16)
+            low = (rest - mid.astype(f32)).astype(bf16)
+            rows_left = left[at, cut(g, quarter)]
+            core_part[at, here] = (
+                jnp.dot(rows_left, hi, preferred_element_type=f32)
+                + jnp.dot(rows_left, mid, preferred_element_type=f32)
+                + jnp.dot(rows_left, low, preferred_element_type=f32)
+            )
+            return carry
+
+        lax.fori_loop(0, 2, multiply, 0)
+
     own_share = cut(c, share)
     cc = []
     for k in range(1, n_cell):
+        core_rows_of(k)
         copy = remote(
             core_part.at[cut(cell_of(k), share), :], core_cell.at[k - 1],
             cc_s.at[k - 1], cc_r.at[k - 1], cell=cell_of(k),
         )
         copy.start()
         cc.append(copy)
+    core_rows_of(0)
     for k in range(1, n_cell):
         cc[k - 1].wait_recv()
         core_part[own_share, :] = core_part[own_share, :] + core_cell[k - 1]
@@ -203,10 +211,11 @@
         copy = remote(core_part.at[src, :], core_gene.at[i], cg_s.at[i], cg_r.at[i], gene=peer)
         copy.start()
         cg.append(copy)
+    send_left(0)
 
     for copy in agz[n_rank - 1 :]:
         copy.wait_recv()
-    for copy in agx:
+    for copy in agx[:-2]:
         copy.wait_recv()
     chunks = dense.shape[1] // GENE_CHUNK
 
@@ -241,38 +250,41 @@
         copy.start()
         cr.append(copy)
 
-    def own_chunk(j, carry):
-        gene_out[:, cut(j, GENE_CHUNK)] = jnp.dot(
-            left[own_share, :], dense[:, cut(j, GENE_CHUNK)], preferred_element_type=f32
-        )
-        return carry
-
-    lax.fori_loop(0, chunks // 2, own_chunk, 0)
-
     final = core_part[own_rows, cut(r, lanes)]
     for k in range(1, n_rank):
         cr[k - 1].wait_recv()
         final = final + core_rank[k - 1]
     out_rows = pl.ds(pl.multiple_of(g * core_rows, 8), core_rows)
     core_out[out_rows, cut(r, lanes)] = final
+    own_piece = core_out.at[out_rows, cut(r, lanes)]
     ar = []
     for k in range(1, n_rank):
-        copy = remote(
-            core_out.at[out_rows, cut(r, lanes)], core_out.at[out_rows, cut(r, lanes)],
-            ar_s.at[k - 1], ar_r.at[k - 1], rank=rank_of(k),
-        )
+        copy = remote(own_piece, own_piece, ar_s.at[k - 1], ar_r.at[k - 1], rank=rank_of(k))
         copy.start()
         ar.append(copy)
-
-    lax.fori_loop(chunks // 2, chunks, own_chunk, 0)
-
-    for copy in ar:
-        copy.wait_recv()
     ag = []
-    for i, peer in enumerate(gene_peers):
-        copy = remote(core_out.at[out_rows, :], core_out.at[out_rows, :], ag_s.at[i], ag_r.at[i], gene=peer)
-        copy.start()
-        ag.append(copy)
+
+    def spread(k):
+        piece = core_out.at[out_rows, cut(rank_of(n_rank - k), lanes)]
+        for i, peer in enumerate(gene_peers):
+            copy = remote(piece, piece, ag_s.at[k, i], ag_r.at[k, i], gene=peer)
+            copy.start()
+            ag.append(copy)
+
+    spread(0)
+    for k in range(1, n_rank):
+        ar[k - 1].wait_recv()
+        spread(k)
+
+    for copy in agx[-2:]:
+        copy.wait_recv()
+
+    def own_chunk(j, carry):
+        here = cut(j, GENE_CHUNK)
+        gene_out[:, here] = jnp.dot(left[own_share, :], dense[:, here], preferred_element_type=f32)
+        return carry
+
+    lax.fori_loop(0, chunks, own_chunk, 0)
 
     for k in range(1, n_cell):
 
@@ -284,6 +296,12 @@
 
         lax.fori_loop(0, chunks, add_chunk, 0)
 
+    for copy in rsz:
+        copy.wait_recv()
+    mine = part[pl.ds(pl.multiple_of(g * quarter + r * shard, shard), shard), :]
+    for j in range(n_rank - 1):
+        mine = mine + hopz[j]
+    right_out[...] = mine
     for copy in ag:
         copy.wait_recv()
 
@@ -333,9 +351,9 @@
         ),
         in_specs=[
             pl.BlockSpec(memory_space=pltpu.SMEM),
-            pl.BlockSpec(memory_space=pl.ANY),
-            pl.BlockSpec(memory_space=pl.ANY),
-            pl.BlockSpec(memory_space=pl.ANY),
+            pl.BlockSpec(memory_space=pltpu.HBM),
+            pl.BlockSpec(memory_space=pltpu.HBM),
+            pl.BlockSpec(memory_space=pltpu.HBM),
         ],
         out_specs=tuple(pl.BlockSpec(memory_space=pltpu.VMEM) for _ in range(3)),
         scratch_shapes=[
@@ -355,7 +373,7 @@
             pltpu.VMEM((n_cell - 1, share, genes), f32),
             dma((4,)),
             *pair(2 * z),
-            *pair(2),
+            *pair(n_cell, 2),
             *pair(4),
             *pair(2 * n_rank),
             *pair(z),
@@ -363,11 +381,11 @@
             *pair(x),
             *pair(z),
             *pair(z),
-            *pair(x),
+            *pair(n_rank, x),
             *pair(n_cell - 1, chunks),
         ],
         compiler_params=pltpu.CompilerParams(
-            collective_id=0, has_side_effects=True, vmem_limit_bytes=62 * 1024 * 1024
+            collective_id=0, has_side_effects=True, vmem_limit_bytes=46 * 1024 * 1024
         ),
         name="sketch",
     )(code, tiles, test_right, test_left.T)

time: 110 us -> 89.5 us (0.81)
  Pallas kernels: 101 us -> 80.7 us
  other arithmetic: 6.57 us -> 3.01 us
  local copies, waits for them, and re-layouts: 1.59 us -> 4.31 us
    pallas_call x1, Pallas kernels: 101 us -> 80.7 us  [body(): pl.pallas_call(functools.partial(kernel, sizes), out_shape=(jax.ShapeDtyp...]
    add x1, other arithmetic: 5.27 us -> 2.22 us  [body(): return (right_mine, gene_sketch_old + gene_sum, core)]
    unnamed x6 -> x8, local copies, waits for them, and re-layouts: 1.59 us -> 4.31 us
where the time goes in v2:
time: 89.5 us; the launch traced here: 89.3 us
  Pallas kernels  80.7 us (90%)
  local copies, waits for them, and re-layouts  4.31 us (5%)
  other arithmetic  3.01 us (3%)
  between operations  1.32 us (1%)
    pallas_call x1, Pallas kernels, body(): pl.pallas_call(functools.partial(kernel, sizes), out_shape=(jax.ShapeDtyp...  80.7 us
    unnamed x8, local copies, waits for them, and re-layouts  4.31 us
    add x1, other arithmetic, body(): return (right_mine, gene_sketch_old + gene_sum, core)  2.22 us

profile of v2, /device:TPU:0, one launch (start us, length us, event | category | flops | bytes accessed | tf_op | source)
XLA Modules:
  0.0 89.3 jit_solution(2827259220444025749)
XLA Ops:
  1.3 0.8 select_reduce_fusion.code
  2.1 0.0 copy-start
  2.1 1.6 %copy-done = bf16[2048,512]{1,0:T(8,128)(2,1)S(1)} copy-done((bf16[2048,512]{1,0:T(8,128)(2,1)S(1)}, bf16[2048,512]{1,0:T(8,128)(2,1)}, u32[]{:S(2)}) %copy-start) | copy-done | bytes 2097176
  3.7 0.0 copy-start.1
  3.7 1.1 %copy-done.1 = bf16[2048,192]{0,1:T(8,128)(2,1)S(1)} copy-done((bf16[2048,192]{0,1:T(8,128)(2,1)S(1)}, bf16[2048,192]{0,1:T(8,128)(2,1)}, u32[]{:S(2)}) %copy-start.1) | copy-done | bytes 786456
  4.8 0.0 copy-start.2
  4.8 80.7 %sketch.1 = (f32[128,512]{1,0:T(8,128)S(1)}, f32[384,2048]{1,0:T(8,128)S(1)}, f32[384,512]{1,0:T(8,128)S(1)}) custom-call(s32[128]{0:T(128)S(1)} %select_reduce_fusion.code, bf16[96,256,128]{2,1,0:T(8,128)(2,1)} %bitcast.6, bf16[2048,512]{1,0:T(8,128)(2,1)S(1)} %copy-done, bf16[192,2048]{1,0:T(8,128)(2,1)S(1)} %bitcast.5), custom_call_target="tpu_custom_call" | custom-call | tf_op jit(solution)/shard_map/sketch/pallas_call | solution.py:345
  85.5 0.0 copy-done.2
  85.5 2.2 %add.16 = f32[384,2048]{1,0:T(8,128)} add(f32[384,2048]{1,0:T(8,128)S(1)} %copy-done.2, f32[384,2048]{1,0:T(8,128)S(1)} %get-tuple-element.7) | non-fusion elementwise | flops 786432 | bytes 9437184 | tf_op jit(solution)/shard_map/add | solution.py:392
  87.8 0.7 copy.12
  88.5 0.9 copy.13
  (2 shorter events, 0.0 us)
Async XLA Ops:
  2.1 1.6 %copy-start = (bf16[2048,512]{1,0:T(8,128)(2,1)S(1)}, bf16[2048,512]{1,0:T(8,128)(2,1)}, u32[]{:S(2)}) copy-start(bf16[2048,512]{1,0:T(8,128)(2,1)} %right_in.1) | copy-start | bytes 6291460
  3.7 1.1 %copy-start.1 = (bf16[2048,192]{0,1:T(8,128)(2,1)S(1)}, bf16[2048,192]{0,1:T(8,128)(2,1)}, u32[]{:S(2)}) copy-start(bf16[2048,192]{0,1:T(8,128)(2,1)} %param.10) | copy-start | bytes 2359300
  4.8 80.7 %copy-start.2 = (f32[384,2048]{1,0:T(8,128)S(1)}, f32[384,2048]{1,0:T(8,128)}, u32[]{:S(2)}) copy-start(f32[384,2048]{1,0:T(8,128)} %param.11) | copy-start | bytes 9437188

commit v3 on v2

--- a/solution.py
+++ b/solution.py
@@ -86,6 +86,14 @@
             )
             copy.start()
             agz.append(copy)
+    agx = []
+    for i, peer in enumerate((gx, gy)):
+        copy = remote(
+            left_in.at[:, cut(g, quarter)], left.at[cut(r, lw), cut(g, quarter)],
+            agx_s.at[n_rank, i], agx_r.at[n_rank, i], gene=peer,
+        )
+        copy.start()
+        agx.append(copy)
     load_tiles.wait()
     load_table.wait()
 
@@ -146,17 +154,21 @@
         copy.wait()
     for copy in agz[: n_rank - 1]:
         copy.wait_recv()
-    agx = []
-
-    def send_left(k):
-        for i, peer in enumerate((gx, gy)):
-            here = left.at[cut(cell_of(k), share), cut(g, quarter)]
-            copy = remote(here, here, agx_s.at[k, i], agx_r.at[k, i], gene=peer)
-            copy.start()
-            agx.append(copy)
-
-    for k in range(1, n_cell):
-        send_left(k)
+    per_share = 0 if n_rank % n_cell else n_rank // n_cell
+    lead = n_rank - per_share
+    base = (c + 1) * per_share
+
+    def left_piece(j, act):
+        z = lax.rem(base + j, n_rank)
+        here = left.at[cut(z, lw), cut(g, quarter)]
+
+        @pl.when(z != r)
+        def _():
+            for i, peer in enumerate((gx, gy)):
+                act(remote(here, here, agx_s.at[j, i], agx_r.at[j, i], gene=peer))
+
+    for j in range(lead):
+        left_piece(j, lambda copy: copy.start())
 
     o0.wait_recv()
     o1.wait_recv()
@@ -169,7 +181,8 @@
         part[here, h1] = part[here, h1] + hop1[3, cut(z, shard), :] + hop2[1, cut(z, shard), :]
         if j < n_rank - 1:
             copy = remote(part.at[here, :], hopz.at[j], rsz_s.at[j], rsz_r.at[j], rank=z)
-            copy.start()
+            if j < n_rank - 2:
+                copy.start()
             rsz.append(copy)
     def core_rows_of(k):
         at = cut(cell_of(k), share)
@@ -211,12 +224,15 @@
         copy = remote(core_part.at[src, :], core_gene.at[i], cg_s.at[i], cg_r.at[i], gene=peer)
         copy.start()
         cg.append(copy)
-    send_left(0)
+    for j in range(lead, n_rank):
+        left_piece(j, lambda copy: copy.start())
 
     for copy in agz[n_rank - 1 :]:
         copy.wait_recv()
-    for copy in agx[:-2]:
+    for copy in agx:
         copy.wait_recv()
+    for j in range(lead):
+        left_piece(j, lambda copy: copy.wait_recv())
     chunks = dense.shape[1] // GENE_CHUNK
 
     def gene_copy(k, j):
@@ -262,6 +278,7 @@
         copy = remote(own_piece, own_piece, ar_s.at[k - 1], ar_r.at[k - 1], rank=rank_of(k))
         copy.start()
         ar.append(copy)
+    rsz[-1].start()
     ag = []
 
     def spread(k):
@@ -276,8 +293,8 @@
         ar[k - 1].wait_recv()
         spread(k)
 
-    for copy in agx[-2:]:
-        copy.wait_recv()
+    for j in range(lead, n_rank):
+        left_piece(j, lambda copy: copy.wait_recv())
 
     def own_chunk(j, carry):
         here = cut(j, GENE_CHUNK)
@@ -307,6 +324,8 @@
 
     for copy in agz + agx + [d0, d1, o0, o1] + second[0] + second[1] + rsz + cc + cg + cr + ar + ag:
         copy.wait_send()
+    for j in range(n_rank):
+        left_piece(j, lambda copy: copy.wait_send())
     for k in range(1, n_cell):
 
         def drain(j, carry):
@@ -373,7 +392,7 @@
             pltpu.VMEM((n_cell - 1, share, genes), f32),
             dma((4,)),
             *pair(2 * z),
-            *pair(n_cell, 2),
+            *pair(n_rank + 1, 2),
             *pair(4),
             *pair(2 * n_rank),
             *pair(z),

time: 89.5 us -> 91 us (1.017)
  the two profiles are of different devices: /device:TPU:0 before, /device:TPU:26 now
where the time goes in v3:
time: 91 us; the launch traced here: 90.8 us
  Pallas kernels  82.2 us (90%)
  local copies, waits for them, and re-layouts  4.31 us (5%)
  other arithmetic  3.01 us (3%)
  between operations  1.32 us (1%)
    pallas_call x1, Pallas kernels, body(): pl.pallas_call(functools.partial(kernel, sizes), out_shape=(jax.ShapeDtyp...  82.2 us
    unnamed x8, local copies, waits for them, and re-layouts  4.31 us
    add x1, other arithmetic, body(): return (right_mine, gene_sketch_old + gene_sum, core)  2.22 us

profile of v3, /device:TPU:26, one launch (start us, length us, event | category | flops | bytes accessed | tf_op | source)
XLA Modules:
  0.0 90.8 jit_solution(10745150311273501094)
XLA Ops:
  1.3 0.8 select_reduce_fusion.code
  2.1 0.0 copy-start
  2.1 1.6 %copy-done = bf16[2048,512]{1,0:T(8,128)(2,1)S(1)} copy-done((bf16[2048,512]{1,0:T(8,128)(2,1)S(1)}, bf16[2048,512]{1,0:T(8,128)(2,1)}, u32[]{:S(2)}) %copy-start) | copy-done | bytes 2097176
  3.7 0.0 copy-start.1
  3.7 1.1 %copy-done.1 = bf16[2048,192]{0,1:T(8,128)(2,1)S(1)} copy-done((bf16[2048,192]{0,1:T(8,128)(2,1)S(1)}, bf16[2048,192]{0,1:T(8,128)(2,1)}, u32[]{:S(2)}) %copy-start.1) | copy-done | bytes 786456
  4.8 0.0 copy-start.2
  4.8 82.2 %sketch.1 = (f32[128,512]{1,0:T(8,128)S(1)}, f32[384,2048]{1,0:T(8,128)S(1)}, f32[384,512]{1,0:T(8,128)S(1)}) custom-call(s32[128]{0:T(128)S(1)} %select_reduce_fusion.code, bf16[96,256,128]{2,1,0:T(8,128)(2,1)} %bitcast.6, bf16[2048,512]{1,0:T(8,128)(2,1)S(1)} %copy-done, bf16[192,2048]{1,0:T(8,128)(2,1)S(1)} %bitcast.5), custom_call_target="tpu_custom_call" | custom-call | tf_op jit(solution)/shard_map/sketch/pallas_call | solution.py:364
  87.0 0.0 copy-done.2
  87.0 2.2 %add.16 = f32[384,2048]{1,0:T(8,128)} add(f32[384,2048]{1,0:T(8,128)S(1)} %copy-done.2, f32[384,2048]{1,0:T(8,128)S(1)} %get-tuple-element.7) | non-fusion elementwise | flops 786432 | bytes 9437184 | tf_op jit(solution)/shard_map/add | solution.py:411
  89.3 0.7 copy.12
  90.0 0.9 copy.13
  (2 shorter events, 0.0 us)
Async XLA Ops:
  2.1 1.6 %copy-start = (bf16[2048,512]{1,0:T(8,128)(2,1)S(1)}, bf16[2048,512]{1,0:T(8,128)(2,1)}, u32[]{:S(2)}) copy-start(bf16[2048,512]{1,0:T(8,128)(2,1)} %right_in.1) | copy-start | bytes 6291460
  3.7 1.1 %copy-start.1 = (bf16[2048,192]{0,1:T(8,128)(2,1)S(1)}, bf16[2048,192]{0,1:T(8,128)(2,1)}, u32[]{:S(2)}) copy-start(bf16[2048,192]{0,1:T(8,128)(2,1)} %param.10) | copy-start | bytes 2359300
  4.8 82.2 %copy-start.2 = (f32[384,2048]{1,0:T(8,128)S(1)}, f32[384,2048]{1,0:T(8,128)}, u32[]{:S(2)}) copy-start(f32[384,2048]{1,0:T(8,128)} %param.11) | copy-start | bytes 9437188

commit v4 on v3

--- a/solution.py
+++ b/solution.py
@@ -66,13 +66,8 @@
     load_table = pltpu.make_async_copy(right_in, table, load_sem.at[1])
     load_tiles.start()
     load_table.start()
-    own_left = []
-    for i, q in enumerate((g, gd)):
-        copy = pltpu.make_async_copy(
-            left_in.at[:, cut(q, quarter)], left.at[cut(r, lw), cut(q, quarter)], load_sem.at[2 + i]
-        )
-        copy.start()
-        own_left.append(copy)
+    own_left = pltpu.make_async_copy(left_in, left.at[cut(r, lw), :], load_sem.at[2])
+    own_left.start()
 
     pl.semaphore_wait(barrier, (n_rank - 1) + len(gene_peers) + (n_cell - 1))
 
@@ -86,14 +81,6 @@
             )
             copy.start()
             agz.append(copy)
-    agx = []
-    for i, peer in enumerate((gx, gy)):
-        copy = remote(
-            left_in.at[:, cut(g, quarter)], left.at[cut(r, lw), cut(g, quarter)],
-            agx_s.at[n_rank, i], agx_r.at[n_rank, i], gene=peer,
-        )
-        copy.start()
-        agx.append(copy)
     load_tiles.wait()
     load_table.wait()
 
@@ -150,8 +137,7 @@
             copies.append(copy)
         second.append(copies)
 
-    for copy in own_left:
-        copy.wait()
+    own_left.wait()
     for copy in agz[: n_rank - 1]:
         copy.wait_recv()
     per_share = 0 if n_rank % n_cell else n_rank // n_cell
@@ -181,8 +167,7 @@
         part[here, h1] = part[here, h1] + hop1[3, cut(z, shard), :] + hop2[1, cut(z, shard), :]
         if j < n_rank - 1:
             copy = remote(part.at[here, :], hopz.at[j], rsz_s.at[j], rsz_r.at[j], rank=z)
-            if j < n_rank - 2:
-                copy.start()
+            copy.start()
             rsz.append(copy)
     def core_rows_of(k):
         at = cut(cell_of(k), share)
@@ -229,8 +214,6 @@
 
     for copy in agz[n_rank - 1 :]:
         copy.wait_recv()
-    for copy in agx:
-        copy.wait_recv()
     for j in range(lead):
         left_piece(j, lambda copy: copy.wait_recv())
     chunks = dense.shape[1] // GENE_CHUNK
@@ -278,7 +261,6 @@
         copy = remote(own_piece, own_piece, ar_s.at[k - 1], ar_r.at[k - 1], rank=rank_of(k))
         copy.start()
         ar.append(copy)
-    rsz[-1].start()
     ag = []
 
     def spread(k):
@@ -322,7 +304,7 @@
     for copy in ag:
         copy.wait_recv()
 
-    for copy in agz + agx + [d0, d1, o0, o1] + second[0] + second[1] + rsz + cc + cg + cr + ar + ag:
+    for copy in agz + [d0, d1, o0, o1] + second[0] + second[1] + rsz + cc + cg + cr + ar + ag:
         copy.wait_send()
     for j in range(n_rank):
         left_piece(j, lambda copy: copy.wait_send())
@@ -390,9 +372,9 @@
             pltpu.VMEM((z, core_rows, lanes), f32),
             pltpu.VMEM((n_cell - 1, share, genes), f32),
             pltpu.VMEM((n_cell - 1, share, genes), f32),
-            dma((4,)),
+            dma((3,)),
             *pair(2 * z),
-            *pair(n_rank + 1, 2),
+            *pair(n_rank, 2),
             *pair(4),
             *pair(2 * n_rank),
             *pair(z),

time: 91 us -> 89.4 us (0.982)
  the two profiles are of different devices: /device:TPU:26 before, /device:TPU:0 now
where the time goes in v4:
time: 89.4 us; the launch traced here: 89.2 us
  Pallas kernels  80.5 us (90%)
  local copies, waits for them, and re-layouts  4.31 us (5%)
  other arithmetic  3.01 us (3%)
  between operations  1.32 us (1%)
    pallas_call x1, Pallas kernels, body(): pl.pallas_call(functools.partial(kernel, sizes), out_shape=(jax.ShapeDtyp...  80.5 us
    unnamed x8, local copies, waits for them, and re-layouts  4.31 us
    add x1, other arithmetic, body(): return (right_mine, gene_sketch_old + gene_sum, core)  2.22 us

profile of v4, /device:TPU:0, one launch (start us, length us, event | category | flops | bytes accessed | tf_op | source)
XLA Modules:
  0.0 89.2 jit_solution(10502631415690441536)
XLA Ops:
  1.3 0.8 select_reduce_fusion.code
  2.1 0.0 copy-start
  2.1 1.6 %copy-done = bf16[2048,512]{1,0:T(8,128)(2,1)S(1)} copy-done((bf16[2048,512]{1,0:T(8,128)(2,1)S(1)}, bf16[2048,512]{1,0:T(8,128)(2,1)}, u32[]{:S(2)}) %copy-start) | copy-done | bytes 2097176
  3.7 0.0 copy-start.1
  3.7 1.1 %copy-done.1 = bf16[2048,192]{0,1:T(8,128)(2,1)S(1)} copy-done((bf16[2048,192]{0,1:T(8,128)(2,1)S(1)}, bf16[2048,192]{0,1:T(8,128)(2,1)}, u32[]{:S(2)}) %copy-start.1) | copy-done | bytes 786456
  4.8 0.0 copy-start.2
  4.8 80.5 %sketch.1 = (f32[128,512]{1,0:T(8,128)S(1)}, f32[384,2048]{1,0:T(8,128)S(1)}, f32[384,512]{1,0:T(8,128)S(1)}) custom-call(s32[128]{0:T(128)S(1)} %select_reduce_fusion.code, bf16[96,256,128]{2,1,0:T(8,128)(2,1)} %bitcast.6, bf16[2048,512]{1,0:T(8,128)(2,1)S(1)} %copy-done, bf16[192,2048]{1,0:T(8,128)(2,1)S(1)} %bitcast.5), custom_call_target="tpu_custom_call" | custom-call | tf_op jit(solution)/shard_map/sketch/pallas_call | solution.py:346
  85.4 0.0 copy-done.2
  85.4 2.2 %add.16 = f32[384,2048]{1,0:T(8,128)} add(f32[384,2048]{1,0:T(8,128)S(1)} %copy-done.2, f32[384,2048]{1,0:T(8,128)S(1)} %get-tuple-element.7) | non-fusion elementwise | flops 786432 | bytes 9437184 | tf_op jit(solution)/shard_map/add | solution.py:393
  87.6 0.7 copy.12
  88.3 0.9 copy.13
  (2 shorter events, 0.0 us)
Async XLA Ops:
  2.1 1.6 %copy-start = (bf16[2048,512]{1,0:T(8,128)(2,1)S(1)}, bf16[2048,512]{1,0:T(8,128)(2,1)}, u32[]{:S(2)}) copy-start(bf16[2048,512]{1,0:T(8,128)(2,1)} %right_in.1) | copy-start | bytes 6291460
  3.7 1.1 %copy-start.1 = (bf16[2048,192]{0,1:T(8,128)(2,1)S(1)}, bf16[2048,192]{0,1:T(8,128)(2,1)}, u32[]{:S(2)}) copy-start(bf16[2048,192]{0,1:T(8,128)(2,1)} %param.10) | copy-start | bytes 2359300
  4.8 80.5 %copy-start.2 = (f32[384,2048]{1,0:T(8,128)S(1)}, f32[384,2048]{1,0:T(8,128)}, u32[]{:S(2)}) copy-start(f32[384,2048]{1,0:T(8,128)} %param.11) | copy-start | bytes 9437188
